TPU v7x, 32 devices: a whole 2x2x4 slice. The times are simulated.
32 devices in a mesh: dp: 8 (over y, x, core), tensor: 4 (over z).
Axes of the slice: x: 2, y: 2, z: 4, core: 2. Of those that a mesh axis runs over, the one named last changes fastest.
Arguments:
- hidden_in: bfloat16 [32, 512, 768], P('dp'), may hold values from -6 to 6
- out_grad: bfloat16 [32, 512, 768], P('dp'), may hold values from -3 to 3
- segment_ids: int32 [32, 512], P('dp'), may hold values from 0 to 7, never falling along the last dimension, each value on 1 to 256 neighbouring positions
- step_count: int32 [1], replicated, may hold values from 1 to 199999
- qkv_state: float32 [3, 768, 3, 768], P(None, 'dp', None, 'tensor'), as said below
- qv_bias_state: float32 [3, 2, 12, 64], P(None, None, 'tensor', 'dp'), as said below
- out_state: float32 [3, 768, 768], P(None, 'tensor', 'dp'), as said below
- up_state: float32 [3, 768, 3072], P(None, 'dp', 'tensor'), as said below
- up_bias_state: float32 [3, 24, 128], P(None, 'tensor', 'dp'), as said below
- down_state: float32 [3, 3072, 768], P(None, 'tensor', 'dp'), as said below
- vector_state: float32 [3, 6, 768], P(None, None, 'dp'), as said below
Outputs:
- hidden_out: bfloat16 [32, 512, 768], P('dp')
- grad_in: bfloat16 [32, 512, 768], P('dp')
- grad_qkv: float32 [768, 3, 768], P('dp', None, 'tensor')
- grad_qv_bias: float32 [2, 12, 64], P(None, 'tensor', 'dp')
- grad_out: float32 [768, 768], P('tensor', 'dp')
- grad_up: float32 [768, 3072], P('dp', 'tensor')
- grad_up_bias: float32 [24, 128], P('tensor', 'dp')
- grad_down: float32 [3072, 768], P('tensor', 'dp')
- grad_vectors: float32 [6, 768], P(None, 'dp')
- new_qkv_state: float32 [2, 768, 3, 768], P(None, 'dp', None, 'tensor')
- new_qv_bias_state: float32 [2, 2, 12, 64], P(None, None, 'tensor', 'dp')
- new_out_state: float32 [2, 768, 768], P(None, 'tensor', 'dp')
- new_up_state: float32 [2, 768, 3072], P(None, 'dp', 'tensor')
- new_up_bias_state: float32 [2, 24, 128], P(None, 'tensor', 'dp')
- new_down_state: float32 [2, 3072, 768], P(None, 'tensor', 'dp')
- new_vector_state: float32 [2, 6, 768], P(None, None, 'dp')
- plan: float32 [3], replicated
Inputs may be any that keep to these rules, and one draw needn't show every extreme that they name: `segment_ids`: within each packed row the fragment numbers never fall; a token attends exactly to the tokens of its own row with the same number. `qkv_state`: index 2 (second moments) is positive. `qv_bias_state`: index 2 (second moments) is positive. `out_state`: index 2 (second moments) is positive. `up_state`: index 2 (second moments) is positive. `up_bias_state`: index 2 (second moments) is positive. `down_state`: index 2 (second moments) is positive. `vector_state`: index 2 (second moments) is positive.
All inputs are finite; a program needn't handle non-finite values.
Results may differ from a plain program's by a relative error of at most 0.023.
The roundings to bfloat16 on the way count: a program that leaves them out, or rounds other values in their place, can miss the bound.
Values may be sent and summed in bfloat16 or wider, within the bound.
No kernel may reach another device: no remote copies, remote signals or barrier semaphores. Data moves between devices by JAX's collectives and lax.ppermute only.
A program may use at most 192 MiB of HBM per device.

v0:
```python
import math
import jax
import jax.numpy as jnp
from jax import lax
from jax.sharding import PartitionSpec as P

HD = 64
norm_eps = 1e-05
beta_first = 0.9
beta_second = 0.999
warm_steps = 10000.0
total_steps = 200000.0


def layer_norm(value, gain, shift):
    center = value - jnp.mean(value, axis=-1, keepdims=True)
    spread = jnp.mean(center * center, axis=-1, keepdims=True)
    return center * lax.rsqrt(spread + norm_eps) * gain + shift


def gelu_exact(value):
    return 0.5 * value * (1.0 + lax.erf(value * 0.7071067811865476))


def scores_of(query, key_rows, segments):
    raw = jnp.einsum(
        "bqhd,bkhd->bhqk", query, key_rows, preferred_element_type=jnp.float32
    ) * HD ** (-0.5)
    same = segments[:, :, None] == segments[:, None, :]
    return jnp.where(same[:, None], raw, -1e30)


def contract_rows(left, right):
    return lax.dot_general(
        left, right, (((0,), (0,)), ((), ())), preferred_element_type=jnp.float32
    )


def contract_cols(left, right):
    return lax.dot_general(
        left, right, (((1,), (1,)), ((), ())), preferred_element_type=jnp.float32
    )


def moment_update(state, grad):
    moment_one = beta_first * state[1] + (1.0 - beta_first) * grad
    moment_two = beta_second * state[2] + (1.0 - beta_second) * grad * grad
    return jnp.stack([moment_one, moment_two])


def body(
    hidden_in,
    out_grad,
    segment_ids,
    step_count,
    qkv_state,
    qv_bias_state,
    out_state,
    up_state,
    up_bias_state,
    down_state,
    vector_state,
):
    bf = jnp.bfloat16
    fl = jnp.float32
    w_qkv, b_qv, w_out, w_up, b_up, w_down, vectors = (
        lax.all_gather(qkv_state[0].astype(bf), "dp", axis=0, tiled=True),
        lax.all_gather(qv_bias_state[0].astype(bf), "dp", axis=2, tiled=True),
        lax.all_gather(out_state[0].astype(bf), "dp", axis=1, tiled=True),
        lax.all_gather(up_state[0].astype(bf), "dp", axis=0, tiled=True),
        lax.all_gather(up_bias_state[0].astype(bf), "dp", axis=1, tiled=True),
        lax.all_gather(down_state[0].astype(bf), "dp", axis=1, tiled=True),
        lax.all_gather(vector_state[0].astype(bf), "dp", axis=1, tiled=True),
    )
    count, length, width_model = hidden_in.shape
    rows = count * length
    heads_local = b_qv.shape[1]
    head_width = heads_local * HD
    ff_local = w_up.shape[1]
    scale = HD ** (-0.5)
    plain = hidden_in.reshape(rows, width_model)
    cotangent = out_grad.reshape(rows, width_model)
    vec = vectors.astype(fl)
    proj = jnp.einsum("td,dcf->tcf", plain, w_qkv, preferred_element_type=fl)
    bias_f = b_qv.astype(fl).reshape(2, head_width)
    bias = jnp.stack([bias_f[0], jnp.zeros((head_width,), fl), bias_f[1]])
    proj_b = (proj + bias[None]).astype(bf)
    heads = proj_b.reshape(count, length, 3, heads_local, HD)
    query = heads[:, :, 0]
    key_rows = heads[:, :, 1]
    value_rows = heads[:, :, 2]
    scores = scores_of(query, key_rows, segment_ids)
    top = jnp.max(scores, axis=-1, keepdims=True)
    expd = jnp.exp(scores - top)
    denom = jnp.sum(expd, axis=-1, keepdims=True)
    log_total = top + jnp.log(denom)
    probs_b = (expd / denom).astype(bf)
    context = (
        jnp.einsum("bhqk,bkhd->bqhd", probs_b, value_rows, preferred_element_type=fl)
        .astype(bf)
        .reshape(rows, head_width)
    )
    attn_part = jnp.dot(context, w_out, preferred_element_type=fl)
    attn = lax.psum(attn_part.astype(jnp.bfloat16), "tensor").astype(jnp.float32)
    first, first_pull = jax.vjp(layer_norm, plain.astype(fl) + attn + vec[4], vec[0], vec[1])
    first_b = first.astype(bf)
    up = jnp.dot(first_b, w_up, preferred_element_type=fl) + b_up.astype(fl).reshape(ff_local)
    act, gelu_pull = jax.vjp(gelu_exact, up)
    act_b = act.astype(bf)
    ffn_part = jnp.dot(act_b, w_down, preferred_element_type=fl)
    ffn = lax.psum(ffn_part.astype(jnp.bfloat16), "tensor").astype(jnp.float32)
    out, second_pull = jax.vjp(layer_norm, first + ffn + vec[5], vec[2], vec[3])
    grad_r2, grad_g2, grad_b2 = second_pull(cotangent.astype(fl))
    grad_ffn = grad_r2.astype(bf)
    grad_down = contract_rows(act_b, grad_ffn)
    grad_act = contract_cols(grad_ffn, w_down)
    grad_up_b = gelu_pull(grad_act)[0].astype(bf)
    grad_wup = contract_rows(first_b, grad_up_b)
    grad_bup = jnp.sum(grad_up_b, axis=0, dtype=fl).reshape(b_up.shape)
    feed_part = contract_cols(grad_up_b, w_up)
    feed_back = lax.psum(feed_part.astype(jnp.bfloat16), "tensor").astype(jnp.float32)
    grad_first = grad_r2 + feed_back.astype(bf).astype(fl)
    grad_r1, grad_g1, grad_b1 = first_pull(grad_first)
    grad_attn = grad_r1.astype(bf)
    grad_wout = contract_rows(context, grad_attn)
    grad_context = (
        contract_cols(grad_attn, w_out).astype(bf).reshape(count, length, heads_local, HD)
    )
    again = scores_of(query, key_rows, segment_ids)
    probs = jnp.exp(again - log_total)
    probs_again = probs.astype(bf)
    grad_probs = jnp.einsum("bqhd,bkhd->bhqk", grad_context, value_rows, preferred_element_type=fl)
    grad_value = jnp.einsum("bhqk,bqhd->bkhd", probs_again, grad_context, preferred_element_type=fl)
    row_dot = jnp.sum(probs * grad_probs, axis=-1, keepdims=True)
    grad_scores = (probs * (grad_probs - row_dot)).astype(bf)
    grad_query = (
        jnp.einsum("bhqk,bkhd->bqhd", grad_scores, key_rows, preferred_element_type=fl) * scale
    )
    grad_key = jnp.einsum("bhqk,bqhd->bkhd", grad_scores, query, preferred_element_type=fl) * scale
    grad_proj = (
        jnp.stack([grad_query, grad_key, grad_value], axis=2)
        .astype(bf)
        .reshape(rows, 3, head_width)
    )
    proj_sums = jnp.sum(grad_proj, axis=0, dtype=fl)
    grad_bqv = jnp.stack([proj_sums[0], proj_sums[2]]).reshape(2, heads_local, HD)
    grad_wqkv = jnp.einsum("td,tcf->dcf", plain, grad_proj, preferred_element_type=fl)
    input_part = jnp.einsum("tcf,dcf->td", grad_proj, w_qkv, preferred_element_type=fl)
    vec_part = jnp.stack(
        [grad_g1, grad_b1, grad_g2, grad_b2, jnp.sum(grad_r1, axis=0), jnp.sum(grad_r2, axis=0)]
    )
    input_back = lax.psum(input_part.astype(jnp.bfloat16), "tensor").astype(jnp.float32)
    grad_in = (grad_r1 + input_back.astype(bf).astype(fl)).astype(bf).reshape(hidden_in.shape)
    hidden_out = out.astype(bf).reshape(hidden_in.shape)
    summed = (
        lax.psum_scatter(grad_wqkv, "dp", scatter_dimension=0, tiled=True),
        lax.psum_scatter(grad_bqv, "dp", scatter_dimension=2, tiled=True),
        lax.psum_scatter(grad_wout, "dp", scatter_dimension=1, tiled=True),
        lax.psum_scatter(grad_wup, "dp", scatter_dimension=0, tiled=True),
        lax.psum_scatter(grad_bup, "dp", scatter_dimension=1, tiled=True),
        lax.psum_scatter(grad_down, "dp", scatter_dimension=1, tiled=True),
        lax.psum_scatter(vec_part, "dp", scatter_dimension=1, tiled=True),
    )
    steps_f = step_count[0].astype(fl)
    factor = jnp.minimum(steps_f / warm_steps, (total_steps - steps_f) / (total_steps - warm_steps))
    fix_first = 1.0 - jnp.exp(steps_f * math.log(beta_first))
    fix_second = 1.0 - jnp.exp(steps_f * math.log(beta_second))
    states = (
        qkv_state,
        qv_bias_state,
        out_state,
        up_state,
        up_bias_state,
        down_state,
        vector_state,
    )
    news = tuple((moment_update(s, g) for s, g in zip(states, summed)))
    plan = jnp.stack([factor, fix_first, fix_second])
    return (
        hidden_out,
        grad_in,
        summed[0],
        summed[1],
        summed[2],
        summed[3],
        summed[4],
        summed[5],
        summed[6],
        news[0],
        news[1],
        news[2],
        news[3],
        news[4],
        news[5],
        news[6],
        plan,
    )


def solution(mesh):
    return jax.shard_map(
        body,
        mesh=mesh,
        in_specs=(
            P("dp", None, None),
            P("dp", None, None),
            P("dp", None),
            P(),
            P(None, "dp", None, "tensor"),
            P(None, None, "tensor", "dp"),
            P(None, "tensor", "dp"),
            P(None, "dp", "tensor"),
            P(None, "tensor", "dp"),
            P(None, "tensor", "dp"),
            P(None, None, "dp"),
        ),
        out_specs=(
            P("dp", None, None),
            P("dp", None, None),
            P("dp", None, "tensor"),
            P(None, "tensor", "dp"),
            P("tensor", "dp"),
            P("dp", "tensor"),
            P("tensor", "dp"),
            P("tensor", "dp"),
            P(None, "dp"),
            P(None, "dp", None, "tensor"),
            P(None, None, "tensor", "dp"),
            P(None, "tensor", "dp"),
            P(None, "dp", "tensor"),
            P(None, "tensor", "dp"),
            P(None, "tensor", "dp"),
            P(None, None, "dp"),
            P(),
        ),
        check_vma=False,
    )
```

profile of v0, /device:TPU:0, one launch (start us, length us, event | category | flops | bytes accessed | tf_op | source)
XLA Modules:
  0.0 760.8 jit_solution(6386560561636301362)
XLA Ops:
  9.0 10.6 %all-gather.1 = bf16[1,2,3,64]{2,1,0,3:T(2,128)(2,1)S(1)} all-gather(bf16[1,2,3,8]{2,1,0,3:T(2,128)(2,1)S(1)} %copy.181), channel_id=3, replica_groups=mesh['dp'=8,'tensor'=4] {'dp'}, dimensions={3}, use_global_device_ids=true | all-gather | bytes 864 | tf_op jit(solution)/shard_map/all_gather | solution.py:68
  22.8 11.3 %all-gather.2 = bf16[1,192,768]{1,0,2:T(2,128)(2,1)} all-gather(bf16[1,192,96]{1,0,2:T(2,128)(2,1)S(1)} %copy.142), channel_id=4, replica_groups=mesh['dp'=8,'tensor'=4] {'dp'}, dimensions={2}, use_global_device_ids=true | all-gather | bytes 331776 | tf_op jit(solution)/shard_map/all_gather | solution.py:69
  38.6 15.8 %all-gather = bf16[1,768,3,192]{3,2,0,1:T(4,128)(2,1)} all-gather(bf16[1,96,3,192]{3,2,0,1:T(4,128)(2,1)} %copy.132), channel_id=2, replica_groups=mesh['dp'=8,'tensor'=4] {'dp'}, dimensions={1}, use_global_device_ids=true | all-gather | bytes 995328 | tf_op jit(solution)/shard_map/all_gather | solution.py:67
  62.9 6.2 reshape.215
  93.2 8.7 %all-gather.5 = bf16[1,6,128]{1,0,2:T(2,128)(2,1)S(1)} all-gather(bf16[1,6,16]{1,0,2:T(2,128)(2,1)} %copy.145), channel_id=7, replica_groups=mesh['dp'=8,'tensor'=4] {'dp'}, dimensions={2}, use_global_device_ids=true | all-gather | bytes 1728 | tf_op jit(solution)/shard_map/all_gather | solution.py:71
  103.2 10.8 %all-gather.3 = bf16[1,6,768]{1,0,2:T(2,128)(2,1)S(1)} all-gather(bf16[1,6,96]{1,0,2:T(2,128)(2,1)S(1)} %copy.185), channel_id=5, replica_groups=mesh['dp'=8,'tensor'=4] {'dp'}, dimensions={2}, use_global_device_ids=true | all-gather | bytes 10368 | tf_op jit(solution)/shard_map/all_gather | solution.py:73
  114.4 13.0 %slice_reduce_fusion.1 = (f32[768]{0:T(1024)S(1)}, f32[768]{0:T(1024)S(1)}, f32[768]{0:T(1024)S(1)}, f32[768]{0:T(1024)S(1)}, f32[768]{0:T(1024)S(1)}, /*index=5*/f32[768]{0:T(1024)S(1)}) fusion(f32[1,6,768]{1,0,2:T(1,128)S(1)} %convert_element_type.169), kind=kLoop, calls=%fused_computation.78 | loop fusion | bytes 36864 | tf_op jit(solution)/shard_map/slice | solution.py:112
  127.4 81.6 %all-reduce.6.cloned.1.call-done = bf16[2048,768]{1,0:T(8,128)(2,1)} async-done(((bf16[2048,768]{1,0:T(8,128)(2,1)}), bf16[2048,768]{1,0:T(8,128)(2,1)}) %all-reduce.6.cloned.1.call-update) | async-done | bytes 3145744 | tf_op jit(solution)/shard_map/psum | solution.py:104
  215.8 7.4 multiply_convert_fusion.1
  223.3 6.2 convolution_convert_fusion.1
  229.7 120.0 %all-reduce.8.cloned.1.call-done = bf16[2048,768]{1,0:T(8,128)(2,1)} async-done(((bf16[2048,768]{1,0:T(8,128)(2,1)}), bf16[2048,768]{1,0:T(8,128)(2,1)}) %all-reduce.8.cloned.1.call-update) | async-done | bytes 3145744 | tf_op jit(solution)/shard_map/psum | solution.py:111
  376.4 8.0 %fusion.60 = f32[768,768]{0,1:T(8,128)} fusion(bf16[2048,768]{1,0:T(8,128)(2,1)} %copy-done.36, f32[2048,768]{1,0:T(8,128)} %copy-done.2, f32[2048]{0:T(1024)S(1)} %negate_multiply_fusion.1), kind=kOutput, calls=%fused_computation.147 | convolution fusion | flops 2419064832 | bytes 11804672 | tf_op jit(solution)/shard_map/dot_general | solution.py:34
  384.5 8.0 %fusion.61 = f32[768,768]{1,0:T(8,128)} fusion(bf16[2048,768]{1,0:T(8,128)(2,1)} %copy-done.35, f32[2048,768]{1,0:T(8,128)} %get-tuple-element.123, f32[768]{0:T(1024)} %copy-done.24, f32[768]{0:T(1024)} %copy-done.22, f32[2048]{0:T(1024)S(1)} %fusion.49), kind=kOutput, calls=%fused_computation.148 | convolution fusion | flops 2422210560 | bytes 11810816 | tf_op jit(solution)/shard_map/dot_general | solution.py:34
  392.8 102.9 %all-reduce.10.cloned.1.call-done = bf16[2048,768]{1,0:T(8,128)(2,1)} async-done(((bf16[2048,768]{1,0:T(8,128)(2,1)}), bf16[2048,768]{1,0:T(8,128)(2,1)}) %all-reduce.10.cloned.1.call-update) | async-done | bytes 3145744 | tf_op jit(solution)/shard_map/psum | solution.py:121
  495.7 8.0 %multiply_reduce_fusion.1 = (f32[768]{0:T(1024)}, f32[2048]{0:T(1024)S(1)}, f32[768]{0:T(1024)}, f32[768]{0:T(1024)}) fusion(f32[2048,768]{1,0:T(8,128)} %get-tuple-element.123, f32[2048]{0:T(1024)S(1)} %fusion.49, bf16[2048,768]{1,0:T(8,128)(2,1)} %all-reduce.10.cloned.1.call-done, f32[2048,768]{1,0:T(8,128)} %copy-done.2, ...), kind=kLoop, calls=%fused_computation.19 | loop fusion | flops 17297152 | bytes 15765504 | tf_op jit(solution)/shard_map/transpose(jvp())/reduce_sum | solution.py:18
  503.7 6.1 fusion.65
  517.6 8.3 %multiply_reduce_fusion = (f32[4,3,512]{2,1,0:T(4,128)S(1)}, f32[4,3,512,512]{2,3,1,0:T(8,128)S(1)}) fusion(f32[4,3,512,512]{2,3,1,0:T(8,128)} %copy-done, f32[4,3,512]{2,1,0:T(4,128)S(1)} %log_add_fusion, bf16[4,512,1,3,64]{1,0,4,3,2:T(4,128)(2,1)} %copy-done.11, bf16[4,512,3,64]{1,0,3,2:T(4,128)(2,1)} %reshape.218), kind=kOutput, calls=%fused_computation.1 | convolution fusion | flops 412084224 | bytes 26787840 | tf_op jit(solution)/shard_map/bqhd,bkhd->bhqk/dot_general | solution.py:132
  526.0 6.9 multiply_convert_fusion
  558.4 7.7 %fusion.17 = bf16[4,512,3,64]{1,3,2,0:T(8,128)(2,1)} fusion(f32[4,3,512,512]{2,3,1,0:T(8,128)} %copy-done, f32[4,3,512]{2,1,0:T(4,128)S(1)} %log_add_fusion, bf16[4,512,3,64]{1,0,3,2:T(4,128)(2,1)} %reshape.218), kind=kOutput, calls=%fused_computation.53 | convolution fusion | flops 409337856 | bytes 14180352 | tf_op jit(solution)/shard_map/bhqk,bqhd->bkhd/dot_general | solution.py:133
  585.8 6.2 bitcast_convert_fusion
  601.6 14.3 %all-reduce = f32[2,3,64]{2,1,0:T(4,128)S(1)} all-reduce(f32[2,3,64]{2,1,0:T(4,128)S(1)} %reshape.220), channel_id=10, replica_groups=mesh['dp'=8,'tensor'=4] {'dp'}, use_global_device_ids=true, to_apply=%region_17.18.clone | all-reduce | flops 384 | bytes 3072
  623.8 19.7 %reduce-scatter.20.cloned.1.call-done = f32[96,576]{1,0:T(8,128)} async-done(((f32[768,576]{1,0:T(8,128)}), f32[96,576]{1,0:T(8,128)}) %reduce-scatter.20.cloned.1.call-update) | async-done | bytes 221200
  644.8 67.8 %all-reduce.12.cloned.1.call-done = bf16[2048,768]{1,0:T(8,128)(2,1)} async-done(((bf16[2048,768]{1,0:T(8,128)(2,1)}), bf16[2048,768]{1,0:T(8,128)(2,1)}) %all-reduce.12.cloned.1.call-update) | async-done | bytes 3145744 | tf_op jit(solution)/shard_map/psum | solution.py:152
  721.0 31.0 %reduce-scatter.26.cloned.1.call-done = f32[96,6]{1,0:T(8,128)} async-done(((f32[768,6]{1,0:T(8,128)}), f32[96,6]{1,0:T(8,128)}) %reduce-scatter.26.cloned.1.call-update) | async-done | bytes 2320
  (220 shorter events, 156.9 us)
Async XLA Ops:
  8.0 49.9 %copy-start.6 = (bf16[4,512,768]{2,1,0:T(8,128)(2,1)S(1)}, bf16[4,512,768]{2,1,0:T(8,128)(2,1)}, u32[]{:S(2)}) copy-start(bf16[4,512,768]{2,1,0:T(8,128)(2,1)} %param.11) | copy-start | bytes 9437188
  8.0 200.9 %all-reduce.6.cloned.1.call-start = ((), (), s32[]{:S(2)}) async-start(), calls=%async_computation.6 | async-start | bytes 6291456 | tf_op jit(solution)/shard_map/psum | solution.py:104
  87.5 128.3 %all-gather.10.cloned.1.call-start = ((), (), s32[]{:S(2)}) async-start(), calls=%async_computation.12 | async-start | bytes 1327104 | tf_op jit(solution)/shard_map/all_gather | solution.py:70
  89.2 134.1 %all-gather.12.cloned.1.call-start = ((), (), s32[]{:S(2)}) async-start(), calls=%async_computation.13 | async-start | bytes 1327104 | tf_op jit(solution)/shard_map/all_gather | solution.py:72
  90.9 258.8 %all-reduce.8.cloned.1.call-start = ((), (), s32[]{:S(2)}) async-start(), calls=%async_computation.7 | async-start | bytes 6291456 | tf_op jit(solution)/shard_map/psum | solution.py:111
  127.3 222.4 %copy-start.22 = (f32[768]{0:T(1024)}, f32[768]{0:T(1024)S(1)}, u32[]{:S(2)}) copy-start(f32[768]{0:T(1024)S(1)} %get-tuple-element.111) | copy-start | bytes 9220
  127.3 222.4 %copy-start.24 = (f32[768]{0:T(1024)}, f32[768]{0:T(1024)S(1)}, u32[]{:S(2)}) copy-start(f32[768]{0:T(1024)S(1)} %get-tuple-element.110) | copy-start | bytes 9220
  229.5 266.2 %all-reduce.10.cloned.1.call-start = ((), (), s32[]{:S(2)}) async-start(), calls=%async_computation.8 | async-start | bytes 6291456 | tf_op jit(solution)/shard_map/psum | solution.py:121
  375.5 222.1 %reduce-scatter.24.cloned.1.call-start = ((), (), s32[]{:S(2)}) async-start(), calls=%async_computation.16 | async-start | bytes 73728
  376.4 241.5 %reduce-scatter.18.cloned.1.call-start = ((), (), s32[]{:S(2)}) async-start(), calls=%async_computation.11 | async-start | bytes 2654208 | tf_op jit(solution)/shard_map/reduce_scatter | solution.py:161
  384.4 235.6 %reduce-scatter.16.cloned.1.call-start = ((), (), s32[]{:S(2)}) async-start(), calls=%async_computation.10 | async-start | bytes 2654208 | tf_op jit(solution)/shard_map/reduce_scatter | solution.py:159
  384.5 111.2 %copy-start.23 = (f32[768]{0:T(1024)S(1)}, f32[768]{0:T(1024)}, u32[]{:S(2)}) copy-start(f32[768]{0:T(1024)} %copy-done.22) | copy-start | bytes 9220
  392.5 111.2 %copy-start.21 = (f32[2048]{0:T(1024)S(1)}, f32[2048]{0:T(1024)}, u32[]{:S(2)}) copy-start(f32[2048]{0:T(1024)} %copy-done.20) | copy-start | bytes 24580
  392.6 229.5 %reduce-scatter.22.cloned.1.call-start = ((), (), s32[]{:S(2)}) async-start(), calls=%async_computation.15 | async-start | bytes 884736
  566.2 77.4 %reduce-scatter.20.cloned.1.call-start = ((), (), s32[]{:S(2)}) async-start(), calls=%async_computation.14 | async-start | bytes 2211840
  584.5 128.0 %all-reduce.12.cloned.1.call-start = ((), (), s32[]{:S(2)}) async-start(), calls=%async_computation.9 | async-start | bytes 6291456 | tf_op jit(solution)/shard_map/psum | solution.py:152
  585.8 15.2 %copy-start.26 = (f32[768]{0:T(1024)S(1)}, f32[768]{0:T(1024)}, u32[]{:S(2)}) copy-start(f32[768]{0:T(1024)} %get-tuple-element.107) | copy-start | bytes 9220
  592.1 31.0 %copy-start.15 = (f32[3,192,96]{2,1,0:T(8,128)S(1)}, f32[3,192,96]{2,1,0:T(8,128)}, u32[]{:S(2)}) copy-start(f32[3,192,96]{2,1,0:T(8,128)} %param.17) | copy-start | bytes 663556
  592.1 159.8 %reduce-scatter.26.cloned.1.call-start = ((), (), s32[]{:S(2)}) async-start(), calls=%async_computation.17 | async-start | bytes 442368
  598.4 119.6 %copy-start.28 = (f32[6,16]{1,0:T(8,128)}, f32[6,16]{1,0:T(8,128)S(1)}, u32[]{:S(2)}) copy-start(f32[6,16]{1,0:T(8,128)S(1)} %copy.176) | copy-start | bytes 1156
  616.6 101.3 %copy-start.30 = (f32[2,3,8]{2,0,1:T(2,128)}, f32[2,3,8]{2,0,1:T(2,128)S(1)}, u32[]{:S(2)}) copy-start(f32[2,3,8]{2,0,1:T(2,128)S(1)} %get-tuple-element.115) | copy-start | bytes 580
  623.1 94.8 %copy-start.14 = (f32[192,96]{1,0:T(8,128)}, f32[192,96]{1,0:T(8,128)S(1)}, u32[]{:S(2)}) copy-start(f32[192,96]{1,0:T(8,128)S(1)} %copy.174) | copy-start | bytes 221188
  644.7 73.2 %copy-start.31 = (f32[1,768]{1,0:T(1,128)S(1)}, f32[1,768]{1,0:T(1,128)}, u32[]{:S(2)}) copy-start(f32[1,768]{1,0:T(1,128)} %reshape.225) | copy-start | bytes 9220
  644.7 108.1 %copy-start.32 = (f32[3,6,96]{2,1,0:T(8,128)S(1)}, f32[3,6,96]{2,1,0:T(8,128)}, u32[]{:S(2)}) copy-start(f32[3,6,96]{2,1,0:T(8,128)} %param.21) | copy-start | bytes 20740
  (27 other events, 149.5 us)
Sparse Core Ops, SparseCore 0:
  87.6 121.2 all-reduce.5
  229.6 120.0 all-reduce.7
  375.6 120.0 all-reduce.9
  592.2 120.2 all-reduce.11
Sparse Core Ops, SparseCore 1:
  90.4 25.2 all-gather.9
  118.0 23.8 all-gather.11
  379.6 32.5 reduce-scatter.23
  416.1 42.2 reduce-scatter.17
  462.2 42.2 reduce-scatter.15
  566.2 33.9 reduce-scatter.21
  603.5 40.0 reduce-scatter.19
  719.0 32.9 reduce-scatter.25
where the time goes:
time: 772 us; the launch traced here: 761 us
  waiting for transfers between devices  423 us (55%)
  matrix products  94.3 us (12%)
  local copies, waits for them, and re-layouts  90.2 us (12%)
  blocking collectives  71.4 us (9%)
  other arithmetic  63 us (8%)
  between operations  17.6 us (2%)
    psum x1, waiting for transfers between devices, body(): ffn = lax.psum(ffn_part.astype(jnp.bfloat16), 'tensor').astype(jnp.float32)  120 us
    psum x1, waiting for transfers between devices, body(): lax.psum(feed_part.astype(jnp.bfloat16), 'tensor').astype(jnp.float32)  103 us
    psum x1, waiting for transfers between devices, body(): lax.psum(attn_part.astype(jnp.bfloat16), 'tensor').astype(jnp.float32)  81.6 us
    psum x1, waiting for transfers between devices, body(): lax.psum(input_part.astype(jnp.bfloat16), 'tensor').astype(jnp.float32)  67.8 us
    unnamed x16, waiting for transfers between devices  50.9 us
    unnamed x98, local copies, waits for them, and re-layouts  29.5 us
    reduce_sum x4, other arithmetic, layer_norm(): center = value - jnp.mean(value, axis=-1, keepdims=True)  18.3 us
    dot_general x2, matrix products, contract_rows(): lax.dot_general(left, right, (((0,), (0,)), ((), ())), preferred_element_...  16 us
  transfers between devices with their start and end apart: 12, of which 6 were waited for; matrix products, arithmetic and copies ran while one was open for 21% of the time, Pallas kernels for 0%

commit v1 on v0

--- a/solution.py
+++ b/solution.py
@@ -61,10 +61,31 @@
     down_state,
     vector_state,
 ):
+
+    def _solve_things(matrix, comm_axis):
+        n_now, x_next, next_value = (
+            lax.axis_size(comm_axis),
+            lax.axis_index(comm_axis),
+            matrix.shape[0],
+        )
+        stack_in = tuple(((pp, (pp + 1) % n_now) for pp in range(n_now)))
+        wide_out = jnp.zeros(
+            (*matrix.shape[:0], n_now * next_value, *matrix.shape[1:]), matrix.dtype
+        )
+        shaped = matrix
+        for hop_no in range(n_now):
+            state_next = (x_next - hop_no) % n_now
+            wide_out = lax.dynamic_update_slice_in_dim(
+                wide_out, shaped, state_next * next_value, axis=0
+            )
+            if hop_no < n_now - 1:
+                shaped = lax.ppermute(shaped, comm_axis, stack_in)
+        return wide_out
+
     bf = jnp.bfloat16
     fl = jnp.float32
     w_qkv, b_qv, w_out, w_up, b_up, w_down, vectors = (
-        lax.all_gather(qkv_state[0].astype(bf), "dp", axis=0, tiled=True),
+        _solve_things(qkv_state[0].astype(bf), "dp"),
         lax.all_gather(qv_bias_state[0].astype(bf), "dp", axis=2, tiled=True),
         lax.all_gather(out_state[0].astype(bf), "dp", axis=1, tiled=True),
         lax.all_gather(up_state[0].astype(bf), "dp", axis=0, tiled=True),

time: 772 us -> 809 us (1.048)
  local copies, waits for them, and re-layouts: 90.2 us -> 121 us
  waiting for transfers between devices: 423 us -> 451 us
  blocking collectives: 71.4 us -> 55.5 us
    ppermute x0 -> x7, waiting for transfers between devices: none -> 27.1 us  [_solve_things(): shaped = lax.ppermute(shaped, comm_axis, stack_in)]
    dynamic_update_slice x0 -> x8, local copies, waits for them, and re-layouts: none -> 18.9 us  [_solve_things(): lax.dynamic_update_slice_in_dim(wide_out, shaped, state_next * next_value...]
    all_gather x1 -> x0, blocking collectives: 15.8 us -> none  [body(): lax.all_gather(qkv_state[0].astype(bf), 'dp', axis=0, tiled=True)]
    ppermute x0 -> x7, local copies, waits for them, and re-layouts: none -> 12 us  [_solve_things(): shaped = lax.ppermute(shaped, comm_axis, stack_in)]
    unnamed x98 -> x106, local copies, waits for them, and re-layouts: 29.5 us -> 31.4 us
  transfers between devices with their start and end apart: 12 -> 19, of which waited for: 6 -> 11; matrix products, arithmetic and copies ran while one was open for 21% -> 24% of each run, Pallas kernels for 0% -> 0%
where the time goes in v1:
time: 809 us; the launch traced here: 805 us
  waiting for transfers between devices  451 us (56%)
  local copies, waits for them, and re-layouts  121 us (15%)
  matrix products  96.3 us (12%)
  other arithmetic  61.6 us (8%)
  blocking collectives  55.5 us (7%)
  between operations  17.8 us (2%)
    psum x1, waiting for transfers between devices, body(): ffn = lax.psum(ffn_part.astype(jnp.bfloat16), 'tensor').astype(jnp.float32)  120 us
    psum x1, waiting for transfers between devices, body(): lax.psum(feed_part.astype(jnp.bfloat16), 'tensor').astype(jnp.float32)  103 us
    psum x1, waiting for transfers between devices, body(): lax.psum(attn_part.astype(jnp.bfloat16), 'tensor').astype(jnp.float32)  82.1 us
    psum x1, waiting for transfers between devices, body(): lax.psum(input_part.astype(jnp.bfloat16), 'tensor').astype(jnp.float32)  67.7 us
    unnamed x16, waiting for transfers between devices  50.9 us
    unnamed x106, local copies, waits for them, and re-layouts  31.4 us
    ppermute x7, waiting for transfers between devices, _solve_things(): shaped = lax.ppermute(shaped, comm_axis, stack_in)  27.1 us
    dynamic_update_slice x8, local copies, waits for them, and re-layouts, _solve_things(): lax.dynamic_update_slice_in_dim(wide_out, shaped, state_next * next_value...  18.9 us
  transfers between devices with their start and end apart: 19, of which 11 were waited for; matrix products, arithmetic and copies ran while one was open for 24% of the time, Pallas kernels for 0%

profile of v1, /device:TPU:0, one launch (start us, length us, event | category | flops | bytes accessed | tf_op | source)
XLA Modules:
  0.0 804.8 jit_solution(4725918898749165559)
XLA Ops:
  37.0 9.9 %all-gather = bf16[1,2,3,64]{2,1,0,3:T(2,128)(2,1)S(1)} all-gather(bf16[1,2,3,8]{2,1,0,3:T(2,128)(2,1)S(1)} %copy.213), channel_id=2, replica_groups=mesh['dp'=8,'tensor'=4] {'dp'}, dimensions={3}, use_global_device_ids=true | all-gather | bytes 864 | tf_op jit(solution)/shard_map/all_gather | solution.py:89
  54.6 12.2 %all-gather.1 = bf16[1,192,768]{1,0,2:T(2,128)(2,1)} all-gather(bf16[1,192,96]{1,0,2:T(2,128)(2,1)S(1)} %copy.174), channel_id=3, replica_groups=mesh['dp'=8,'tensor'=4] {'dp'}, dimensions={2}, use_global_device_ids=true | all-gather | bytes 331776 | tf_op jit(solution)/shard_map/all_gather | solution.py:90
  105.8 6.2 reshape.215
  136.7 9.4 %all-gather.4 = bf16[1,6,128]{1,0,2:T(2,128)(2,1)S(1)} all-gather(bf16[1,6,16]{1,0,2:T(2,128)(2,1)} %copy.177), channel_id=6, replica_groups=mesh['dp'=8,'tensor'=4] {'dp'}, dimensions={2}, use_global_device_ids=true | all-gather | bytes 1728 | tf_op jit(solution)/shard_map/all_gather | solution.py:92
  147.4 9.8 %all-gather.2 = bf16[1,6,768]{1,0,2:T(2,128)(2,1)S(1)} all-gather(bf16[1,6,96]{1,0,2:T(2,128)(2,1)S(1)} %copy.217), channel_id=4, replica_groups=mesh['dp'=8,'tensor'=4] {'dp'}, dimensions={2}, use_global_device_ids=true | all-gather | bytes 10368 | tf_op jit(solution)/shard_map/all_gather | solution.py:94
  157.6 13.0 %slice_reduce_fusion.1 = (f32[768]{0:T(1024)S(1)}, f32[768]{0:T(1024)S(1)}, f32[768]{0:T(1024)S(1)}, f32[768]{0:T(1024)S(1)}, f32[768]{0:T(1024)S(1)}, /*index=5*/f32[768]{0:T(1024)S(1)}) fusion(f32[1,6,768]{1,0,2:T(1,128)S(1)} %convert_element_type.173), kind=kLoop, calls=%fused_computation.78 | loop fusion | bytes 36864 | tf_op jit(solution)/shard_map/slice | solution.py:133
  170.6 82.1 %all-reduce.6.cloned.1.call-done = bf16[2048,768]{1,0:T(8,128)(2,1)} async-done(((bf16[2048,768]{1,0:T(8,128)(2,1)}), bf16[2048,768]{1,0:T(8,128)(2,1)}) %all-reduce.6.cloned.1.call-update) | async-done | bytes 3145744 | tf_op jit(solution)/shard_map/psum | solution.py:125
  259.5 7.4 multiply_convert_fusion.1
  266.9 6.2 convolution_convert_fusion.1
  273.2 120.2 %all-reduce.8.cloned.1.call-done = bf16[2048,768]{1,0:T(8,128)(2,1)} async-done(((bf16[2048,768]{1,0:T(8,128)(2,1)}), bf16[2048,768]{1,0:T(8,128)(2,1)}) %all-reduce.8.cloned.1.call-update) | async-done | bytes 3145744 | tf_op jit(solution)/shard_map/psum | solution.py:132
  407.6 5.9 convert_reduce_fusion.1
  420.2 8.0 fusion.61
  428.3 8.0 fusion.62
  436.4 103.1 %all-reduce.10.cloned.1.call-done = bf16[2048,768]{1,0:T(8,128)(2,1)} async-done(((bf16[2048,768]{1,0:T(8,128)(2,1)}), bf16[2048,768]{1,0:T(8,128)(2,1)}) %all-reduce.10.cloned.1.call-update) | async-done | bytes 3145744 | tf_op jit(solution)/shard_map/psum | solution.py:142
  539.6 8.2 %multiply_reduce_fusion.1 = (f32[768]{0:T(1024)}, f32[2048]{0:T(1024)S(1)}, f32[768]{0:T(1024)}, f32[768]{0:T(1024)}) fusion(f32[2048,768]{1,0:T(8,128)} %get-tuple-element.123, f32[2048]{0:T(1024)S(1)} %fusion.50, bf16[2048,768]{1,0:T(8,128)(2,1)} %all-reduce.10.cloned.1.call-done, f32[2048,768]{1,0:T(8,128)} %copy-done.2, ...), kind=kLoop, calls=%fused_computation.19 | loop fusion | flops 17297152 | bytes 15765504 | tf_op jit(solution)/shard_map/transpose(jvp())/reduce_sum | solution.py:18
  547.8 6.1 fusion.66
  561.6 8.3 %multiply_reduce_fusion = (f32[4,3,512]{2,1,0:T(4,128)S(1)}, f32[4,3,512,512]{2,3,1,0:T(8,128)S(1)}) fusion(f32[4,3,512,512]{2,3,1,0:T(8,128)} %copy-done, f32[4,3,512]{2,1,0:T(4,128)S(1)} %log_add_fusion, bf16[4,512,1,3,64]{1,0,4,3,2:T(4,128)(2,1)} %copy-done.11, bf16[4,512,3,64]{1,0,3,2:T(4,128)(2,1)} %reshape.218), kind=kOutput, calls=%fused_computation.1 | convolution fusion | flops 412084224 | bytes 26787840 | tf_op jit(solution)/shard_map/bqhd,bkhd->bhqk/dot_general | solution.py:153
  570.0 6.9 multiply_convert_fusion
  602.3 7.7 fusion.18
  629.8 6.2 bitcast_convert_fusion
  645.6 14.3 %all-reduce = f32[2,3,64]{2,1,0:T(4,128)S(1)} all-reduce(f32[2,3,64]{2,1,0:T(4,128)S(1)} %reshape.220), channel_id=9, replica_groups=mesh['dp'=8,'tensor'=4] {'dp'}, use_global_device_ids=true, to_apply=%region_17.18.clone | all-reduce | flops 384 | bytes 3072
  667.8 19.7 %reduce-scatter.20.cloned.1.call-done = f32[96,576]{1,0:T(8,128)} async-done(((f32[768,576]{1,0:T(8,128)}), f32[96,576]{1,0:T(8,128)}) %reduce-scatter.20.cloned.1.call-update) | async-done | bytes 221200
  688.8 67.7 %all-reduce.12.cloned.1.call-done = bf16[2048,768]{1,0:T(8,128)(2,1)} async-done(((bf16[2048,768]{1,0:T(8,128)(2,1)}), bf16[2048,768]{1,0:T(8,128)(2,1)}) %all-reduce.12.cloned.1.call-update) | async-done | bytes 3145744 | tf_op jit(solution)/shard_map/psum | solution.py:173
  765.0 31.0 %reduce-scatter.26.cloned.1.call-done = f32[96,6]{1,0:T(8,128)} async-done(((f32[768,6]{1,0:T(8,128)}), f32[96,6]{1,0:T(8,128)}) %reduce-scatter.26.cloned.1.call-update) | async-done | bytes 2320
  (255 shorter events, 209.7 us)
Async XLA Ops:
  8.0 244.6 %all-reduce.6.cloned.1.call-start = ((), (), s32[]{:S(2)}) async-start(), calls=%async_computation.6 | async-start | bytes 6291456 | tf_op jit(solution)/shard_map/psum | solution.py:125
  9.2 6.2 collective-permute-start
  16.1 5.5 collective-permute-start.1
  22.2 5.5 collective-permute-start.2
  28.4 5.5 collective-permute-start.3
  33.8 13.0 %collective-permute-start.4 = (bf16[96,3,192]{2,0,1:T(8,128)(2,1)S(1)}, bf16[96,3,192]{2,0,1:T(8,128)(2,1)}, u32[]{:S(2)}, u32[]{:S(2)}) collective-permute-start(bf16[96,3,192]{2,0,1:T(8,128)(2,1)S(1)} %collective-permute-done.3), channel_id=1, source_target_pairs={{0,4},{4,8},{8,12},{12,16},{16,20},{20,24},{24,28},{28,0},{1,5},{5... | collective-permute-start | bytes 331784 | tf_op jit(solution)/shard_map/ppermute | solution.py:82
  46.8 5.8 collective-permute-start.5
  52.6 44.3 %collective-permute-start.6 = (bf16[96,3,192]{2,0,1:T(8,128)(2,1)}, bf16[96,3,192]{2,0,1:T(8,128)(2,1)}, u32[]{:S(2)}, u32[]{:S(2)}) collective-permute-start(bf16[96,3,192]{2,0,1:T(8,128)(2,1)} %collective-permute-done.5), channel_id=1, source_target_pairs={{0,4},{4,8},{8,12},{12,16},{16,20},{20,24},{24,28},{28,0},{1,5},{5... | collective-permute-start | bytes 331784 | tf_op jit(solution)/shard_map/ppermute | solution.py:82
  131.0 128.5 %all-gather.9.cloned.1.call-start = ((), (), s32[]{:S(2)}) async-start(), calls=%async_computation.12 | async-start | bytes 1327104 | tf_op jit(solution)/shard_map/all_gather | solution.py:91
  132.7 134.3 %all-gather.11.cloned.1.call-start = ((), (), s32[]{:S(2)}) async-start(), calls=%async_computation.13 | async-start | bytes 1327104 | tf_op jit(solution)/shard_map/all_gather | solution.py:93
  134.4 259.0 %all-reduce.8.cloned.1.call-start = ((), (), s32[]{:S(2)}) async-start(), calls=%async_computation.7 | async-start | bytes 6291456 | tf_op jit(solution)/shard_map/psum | solution.py:132
  170.6 222.8 %copy-start.26 = (f32[768]{0:T(1024)}, f32[768]{0:T(1024)S(1)}, u32[]{:S(2)}) copy-start(f32[768]{0:T(1024)S(1)} %get-tuple-element.111) | copy-start | bytes 9220
  170.6 222.8 %copy-start.28 = (f32[768]{0:T(1024)}, f32[768]{0:T(1024)S(1)}, u32[]{:S(2)}) copy-start(f32[768]{0:T(1024)S(1)} %get-tuple-element.110) | copy-start | bytes 9220
  273.2 266.4 %all-reduce.10.cloned.1.call-start = ((), (), s32[]{:S(2)}) async-start(), calls=%async_computation.8 | async-start | bytes 6291456 | tf_op jit(solution)/shard_map/psum | solution.py:142
  419.3 222.2 %reduce-scatter.24.cloned.1.call-start = ((), (), s32[]{:S(2)}) async-start(), calls=%async_computation.16 | async-start | bytes 73728
  420.2 241.7 %reduce-scatter.18.cloned.1.call-start = ((), (), s32[]{:S(2)}) async-start(), calls=%async_computation.11 | async-start | bytes 2654208 | tf_op jit(solution)/shard_map/reduce_scatter | solution.py:182
  428.2 235.8 %reduce-scatter.16.cloned.1.call-start = ((), (), s32[]{:S(2)}) async-start(), calls=%async_computation.10 | async-start | bytes 2654208 | tf_op jit(solution)/shard_map/reduce_scatter | solution.py:180
  428.3 111.2 %copy-start.27 = (f32[768]{0:T(1024)S(1)}, f32[768]{0:T(1024)}, u32[]{:S(2)}) copy-start(f32[768]{0:T(1024)} %copy-done.26) | copy-start | bytes 9220
  436.4 111.4 %copy-start.25 = (f32[2048]{0:T(1024)S(1)}, f32[2048]{0:T(1024)}, u32[]{:S(2)}) copy-start(f32[2048]{0:T(1024)} %copy-done.24) | copy-start | bytes 24580
  436.4 229.7 %reduce-scatter.22.cloned.1.call-start = ((), (), s32[]{:S(2)}) async-start(), calls=%async_computation.15 | async-start | bytes 884736
  610.1 77.4 %reduce-scatter.20.cloned.1.call-start = ((), (), s32[]{:S(2)}) async-start(), calls=%async_computation.14 | async-start | bytes 2211840
  628.5 128.0 %all-reduce.12.cloned.1.call-start = ((), (), s32[]{:S(2)}) async-start(), calls=%async_computation.9 | async-start | bytes 6291456 | tf_op jit(solution)/shard_map/psum | solution.py:173
  636.1 159.8 %reduce-scatter.26.cloned.1.call-start = ((), (), s32[]{:S(2)}) async-start(), calls=%async_computation.17 | async-start | bytes 442368
  642.4 119.6 %copy-start.32 = (f32[6,16]{1,0:T(8,128)}, f32[6,16]{1,0:T(8,128)S(1)}, u32[]{:S(2)}) copy-start(f32[6,16]{1,0:T(8,128)S(1)} %copy.208) | copy-start | bytes 1156
  (38 other events, 689.7 us)
Sparse Core Ops, SparseCore 0:
  131.1 121.5 all-reduce.5
  273.3 120.0 all-reduce.7
  419.5 120.0 all-reduce.9
  636.2 120.2 all-reduce.11
Sparse Core Ops, SparseCore 1:
  133.9 25.4 all-gather.8
  161.7 23.8 all-gather.10
  423.4 32.5 reduce-scatter.23
  459.9 42.2 reduce-scatter.17
  506.1 42.2 reduce-scatter.15
  610.2 33.9 reduce-scatter.21
  647.4 40.1 reduce-scatter.19
  763.0 32.9 reduce-scatter.25
